TPU v7x, 256 devices: a whole 4x4x8 slice. The times are simulated.
256 devices in a mesh: seq: 32 (over y, z), tp: 8 (over x, core).
Axes of the slice: x: 4, y: 4, z: 8, core: 2. Of those that a mesh axis runs over, the one named last changes fastest.
Arguments:
- tokens: bfloat16 [16384, 4096], P('seq', 'tp'), may hold values from -40 to 40, as said below
- w_query: bfloat16 [4096, 2048], P(None, 'tp'), may hold values from -0.09375 to 0.09375
- w_key: bfloat16 [4096, 2048], P(None, 'tp'), may hold values from -0.09375 to 0.09375
- w_value: bfloat16 [4096, 2048], P(None, 'tp'), may hold values from -0.09375 to 0.09375
- w_gate: bfloat16 [4096, 2048], P(None, 'tp'), may hold values from -0.09375 to 0.09375
- w_out: bfloat16 [2048, 4096], P(None, 'tp'), may hold values from -0.125 to 0.125
- decay_rate: float32 [16], replicated, may hold values from 1.8310547e-05 to 0.0333333333, as said below
- state_in: float32 [16, 128, 128], P('tp'), may hold values from -192 to 192
Outputs:
- layer_out: bfloat16 [16384, 4096], P('seq', 'tp')
Inputs may be any that keep to these rules, and one draw needn't show every extreme that they name: tokens have scales that vary by row and by column. `decay_rate`: each head either forgets within a few tens of positions or keeps its state over the whole slab.
All inputs are finite; a program needn't handle non-finite values.
Results may differ from a plain program's by a relative error of at most 0.0033.
Values may be sent and summed in bfloat16 or wider, within the bound.
A program may use at most 64 MiB of HBM per device.

v0:
```python
import jax
import jax.numpy as jnp
from jax import lax
from jax.sharding import PartitionSpec as P


def per_device(tokens, w_query, w_key, w_value, w_gate, w_out, decay_rate, state_in):
    hi = lax.Precision.HIGHEST
    row_count = tokens.shape[0]
    width_all = w_query.shape[0]
    heads_here = state_in.shape[0]
    head_dim = state_in.shape[1]
    tp_index = lax.axis_index("tp")
    seq_index = lax.axis_index("seq")
    weight_set = (w_query, w_key, w_value, w_gate)
    gathered = lax.all_gather(tokens, "tp", axis=1, tiled=True)
    gathered_f = gathered.astype(jnp.float32)
    square_sum = jnp.sum(gathered_f * gathered_f, axis=1, keepdims=True)
    raw_set = tuple(
        (jnp.dot(gathered, weight, preferred_element_type=jnp.float32) for weight in weight_set)
    )
    inv_rms = lax.rsqrt(square_sum / float(width_all) + 1e-06)

    def to_heads(array):
        return array.reshape(row_count, heads_here, head_dim).transpose(1, 0, 2)

    query_h = to_heads(jax.nn.silu(raw_set[0] * inv_rms).astype(jnp.bfloat16))
    key_h = to_heads(jax.nn.silu(raw_set[1] * inv_rms).astype(jnp.bfloat16))
    value_h = to_heads((raw_set[2] * inv_rms).astype(jnp.bfloat16))
    gate = jax.nn.silu(raw_set[3] * inv_rms)
    rate_here = lax.dynamic_slice_in_dim(decay_rate, tp_index * heads_here, heads_here)
    rate_col = rate_here[:, None]
    positions = jnp.arange(row_count).astype(jnp.float32)
    lower = positions[:, None] >= positions[None, :]
    gap_mask = jnp.where(lower, positions[:, None] - positions[None, :], 0.0)
    scores = jnp.einsum("hid,hjd->hij", query_h, key_h, preferred_element_type=jnp.float32)
    mask = jnp.where(lower[None], jnp.exp(-rate_col[:, :, None] * gap_mask[None]), 0.0)
    weights = (scores * mask).astype(jnp.bfloat16)
    intra = jnp.einsum("hij,hje->hie", weights, value_h, preferred_element_type=jnp.float32)
    value_f = value_h.astype(jnp.float32)
    tail_decay = jnp.exp(-rate_col * (row_count - 1.0 - positions[None, :]))
    local_state = jnp.einsum(
        "hid,hie->hde", key_h.astype(jnp.float32) * tail_decay[:, :, None], value_f, precision=hi
    )
    piece = lax.all_gather(
        local_state[None].astype(jnp.bfloat16), "seq", axis=0, tiled=True
    ).astype(jnp.float32)
    count = piece.shape[0]
    source = jnp.arange(count)
    distance = seq_index - 1 - source
    exponent = (row_count * jnp.maximum(distance, 0)).astype(jnp.float32)
    factor = jnp.where(
        distance[:, None] >= 0, jnp.exp(-rate_here[None, :] * exponent[:, None]), 0.0
    )
    prefix = jnp.zeros_like(local_state) + jnp.sum(factor[:, :, None, None] * piece, axis=0)
    offset = (row_count * seq_index).astype(jnp.float32)
    incoming = prefix + jnp.exp(-rate_here * offset)[:, None, None] * state_in
    lead_decay = jnp.exp(-rate_col * (positions[None, :] + 1.0))
    inter = jnp.einsum(
        "hid,hde->hie", query_h.astype(jnp.float32) * lead_decay[:, :, None], incoming, precision=hi
    )
    attended = intra + inter
    norm_inv = lax.rsqrt(jnp.mean(attended * attended, axis=2, keepdims=True) + 1e-06)
    normed = (attended * norm_inv).transpose(1, 0, 2).reshape(row_count, heads_here * head_dim)
    hidden = (normed * gate).astype(jnp.bfloat16)
    branch = jnp.dot(
        lax.all_gather(hidden, "tp", axis=1, tiled=True), w_out, preferred_element_type=jnp.float32
    )
    return (tokens.astype(jnp.float32) + branch).astype(jnp.bfloat16)


def solution(mesh):
    return jax.shard_map(
        per_device,
        mesh=mesh,
        in_specs=(
            P("seq", "tp"),
            P(None, "tp"),
            P(None, "tp"),
            P(None, "tp"),
            P(None, "tp"),
            P(None, "tp"),
            P(),
            P("tp", None, None),
        ),
        out_specs=P("seq", "tp"),
        check_vma=False,
    )
```

profile of v0, /device:TPU:1, one launch (start us, length us, event | category | flops | bytes accessed | tf_op | source)
XLA Modules:
  0.0 186.8 jit_solution(16274440902370304356)
XLA Ops:
  6.5 0.0 copy-start
  6.5 0.0 all-gather.5.cloned.1.call-start
  6.5 0.7 all-gather.5.cloned.1.call-update
  7.3 0.0 all-gather.9.cloned.1.call-start
  7.3 1.3 multiply_exponential_fusion.2
  8.6 0.0 copy-start.7
  8.6 0.7 multiply_exponential_fusion
  9.3 38.8 %all-gather.5.cloned.1.call-done = bf16[512,4096]{1,0:T(8,128)(2,1)} async-done(((bf16[512,512]{1,0:T(8,128)(2,1)}), bf16[512,4096]{1,0:T(8,128)(2,1)}) %all-gather.5.cloned.1.call-update) | async-done | bytes 4194320 | tf_op jit(solution)/shard_map/all_gather | solution.py:16
  48.1 0.0 copy-start.1
  48.1 3.2 %multiply_reduce_fusion = f32[512]{0:T(512)S(1)} fusion(bf16[512,4096]{1,0:T(8,128)(2,1)} %all-gather.5.cloned.1.call-done), kind=kLoop, calls=%fused_computation | loop fusion | flops 6290944 | bytes 4196352 | tf_op jit(solution)/shard_map/reduce_sum | solution.py:18
  51.3 0.2 copy-done.1
  51.5 0.0 copy-start.9
  51.5 2.9 %fusion.4 = bf16[512,256]{0,1:T(8,128)(2,1)S(1)} fusion(bf16[512,4096]{1,0:T(8,128)(2,1)S(1)} %copy-done.1, bf16[4096,256]{1,0:T(8,128)(2,1)} %param.11, f32[512]{0:T(512)S(1)} %add_rsqrt_fusion), kind=kOutput, calls=%fused_computation.12 | convolution fusion | flops 1074003968 | bytes 6555648 | tf_op jit(solution)/shard_map/dot_general | solution.py:20
  54.5 0.0 copy-start.4
  54.5 0.2 copy.15
  54.6 4.2 %multiply_convert_fusion.1 = bf16[512,256]{0,1:T(8,128)(2,1)S(1)} fusion(bf16[512,4096]{1,0:T(8,128)(2,1)} %all-gather.5.cloned.1.call-done, bf16[4096,256]{1,0:T(8,128)(2,1)} %param.10, f32[512]{0:T(512)S(1)} %add_rsqrt_fusion), kind=kOutput, calls=%fused_computation.29 | convolution fusion | flops 1074528256 | bytes 6555648 | tf_op jit(solution)/shard_map/dot_general | solution.py:20
  58.9 0.0 copy-done.4
  58.9 0.0 copy-start.3
  58.9 0.7 copy-done.3
  59.6 1.0 convolution_convert_fusion
  60.6 0.0 all-gather.9.cloned.1.call-update
  60.7 0.0 all-gather.7.cloned.1.call-start
  60.8 0.0 copy-done.7
  60.8 0.1 exponential_select_fusion
  60.9 0.9 broadcast_compare_fusion
  61.8 0.2 subtract_select_fusion
  62.0 0.0 copy-done.9
  62.0 5.0 %multiply_convert_fusion.2 = bf16[512,256]{0,1:T(8,128)(2,1)} fusion(bf16[512,4096]{1,0:T(8,128)(2,1)} %all-gather.5.cloned.1.call-done, bf16[4096,256]{1,0:T(8,128)(2,1)} %param.9, f32[512]{0:T(512)S(1)} %add_rsqrt_fusion), kind=kOutput, calls=%fused_computation.30 | convolution fusion | flops 1074528256 | bytes 6555648 | tf_op jit(solution)/shard_map/dot_general | solution.py:20
  66.9 0.0 copy-start.5
  66.9 1.2 copy.14
  68.1 66.4 %all-gather.9.cloned.1.call-done = bf16[64,128,128]{2,1,0:T(8,128)(2,1)} async-done(((bf16[2,128,128]{2,1,0:T(8,128)(2,1)}), bf16[64,128,128]{2,1,0:T(8,128)(2,1)}) %all-gather.9.cloned.1.call-update) | async-done | bytes 2097168 | tf_op jit(solution)/shard_map/all_gather | solution.py:45
  134.4 0.0 copy-start.6
  134.4 0.0 copy-start.8
  134.5 2.1 %fusion = f32[2,128,128]{2,1,0:T(8,128)S(1)} fusion(bf16[32,2,128,128]{3,2,1,0:T(8,128)(2,1)} %bitcast.42, f32[32,2]{1,0:T(8,128)S(1)} %exponential_select_fusion), kind=kLoop, calls=%fused_computation.2 | loop fusion | flops 3112960 | bytes 2228480 | tf_op jit(solution)/shard_map/reduce_sum | solution.py:55
  136.5 0.0 copy-done.5
  136.5 0.0 copy-done.6
  136.5 0.0 copy-done.8
  136.6 1.6 fusion.12
  138.1 3.0 %multiply_reduce_fusion.1 = (f32[2,512]{1,0:T(2,128)S(1)}, f32[2,512,128]{1,2,0:T(8,128)}) fusion(f32[2,512,128]{1,2,0:T(8,128)} %fusion.12, bf16[2,512,128]{1,2,0:T(8,128)(2,1)} %bitcast.46, bf16[2,512,128]{1,2,0:T(8,128)(2,1)} %bitcast.44, f32[512,512]{1,0:T(8,128)S(1)} %subtract_select_fusion, f32[2]{0:T(128)} %copy-done.7, ...), kind=kOutput, calls=%fused_computation.22 | convolution fusion | flops 270924800 | bytes 3149832 | tf_op jit(solution)/shard_map/hij,hje->hie/dot_general | solution.py:39
  141.1 1.1 bitcast_multiply_fusion.1
  142.2 0.0 copy-done.10
  142.2 0.0 copy-start.2
  142.3 5.0 %fusion.9 = bf16[512,256]{0,1:T(8,128)(2,1)} fusion(f32[512,2,128]{0,2,1:T(8,128)S(1)} %bitcast_multiply_fusion.1, bf16[512,4096]{1,0:T(8,128)(2,1)} %all-gather.5.cloned.1.call-done, bf16[4096,256]{1,0:T(8,128)(2,1)} %param.12, f32[512]{0:T(512)S(1)} %copy-done.10), kind=kOutput, calls=%fused_computation.20 | convolution fusion | flops 1074659328 | bytes 7079936 | tf_op jit(solution)/shard_map/dot_general | solution.py:20
  147.3 0.0 all-gather.7.cloned.1.call-update
  147.3 29.4 %all-gather.7.cloned.1.call-done = bf16[512,2048]{0,1:T(8,128)(2,1)} async-done(((bf16[512,256]{0,1:T(8,128)(2,1)}), bf16[512,2048]{0,1:T(8,128)(2,1)}) %all-gather.7.cloned.1.call-update) | async-done | bytes 2097168 | tf_op jit(solution)/shard_map/all_gather | solution.py:67
  176.6 0.0 copy-done
  176.6 0.0 copy-done.2
  176.6 3.7 %fusion.2 = bf16[512,512]{1,0:T(8,128)(2,1)} fusion(bf16[512,2048]{0,1:T(8,128)(2,1)} %all-gather.7.cloned.1.call-done, bf16[2048,512]{1,0:T(8,128)(2,1)S(1)} %copy-done, bf16[512,512]{1,0:T(8,128)(2,1)S(1)} %copy-done.2), kind=kOutput, calls=%fused_computation.6 | convolution fusion | flops 1074528256 | bytes 5242880 | tf_op jit(solution)/shard_map/dot_general | solution.py:66
  (7 shorter events, 0.0 us)
Async XLA Ops:
  6.5 170.1 %copy-start = (bf16[2048,512]{1,0:T(8,128)(2,1)S(1)}, bf16[2048,512]{1,0:T(8,128)(2,1)}, u32[]{:S(2)}) copy-start(bf16[2048,512]{1,0:T(8,128)(2,1)} %param.13) | copy-start | bytes 6291460
  6.5 41.5 %all-gather.5.cloned.1.call-start = ((), (), s32[]{:S(2)}) async-start(), calls=%async_computation | async-start | bytes 4718592 | tf_op jit(solution)/shard_map/all_gather | solution.py:16
  7.3 127.2 %all-gather.9.cloned.1.call-start = ((), (), s32[]{:S(2)}) async-start(), calls=%async_computation.2 | async-start | bytes 2162688 | tf_op jit(solution)/shard_map/all_gather | solution.py:45
  8.6 52.2 %copy-start.7 = (f32[2]{0:T(128)}, f32[2]{0:T(128)S(1)}, u32[]{:S(2)}) copy-start(f32[2]{0:T(128)S(1)} %get-tuple-element.6) | copy-start | bytes 28
  48.1 3.4 %copy-start.1 = (bf16[512,4096]{1,0:T(8,128)(2,1)S(1)}, bf16[512,4096]{1,0:T(8,128)(2,1)}, u32[]{:S(2)}) copy-start(bf16[512,4096]{1,0:T(8,128)(2,1)} %all-gather.5.cloned.1.call-done) | copy-start | bytes 12582916
  51.5 10.4 %copy-start.9 = (f32[512]{0:T(512)}, f32[512]{0:T(512)S(1)}, u32[]{:S(2)}) copy-start(f32[512]{0:T(512)S(1)} %add_rsqrt_fusion) | copy-start | bytes 6148
  54.5 4.4 %copy-start.4 = (bf16[512,256]{0,1:T(8,128)(2,1)}, bf16[512,256]{0,1:T(8,128)(2,1)S(1)}, u32[]{:S(2)}) copy-start(bf16[512,256]{0,1:T(8,128)(2,1)S(1)} %fusion.4) | copy-start | bytes 786436
  58.9 0.7 copy-start.3
  60.7 116.0 %all-gather.7.cloned.1.call-start = ((), (), s32[]{:S(2)}) async-start(), calls=%async_computation.1 | async-start | bytes 2359296 | tf_op jit(solution)/shard_map/all_gather | solution.py:67
  66.9 69.6 %copy-start.5 = (f32[2,128,128]{2,1,0:T(8,128)S(1)}, f32[2,128,128]{2,1,0:T(8,128)}, u32[]{:S(2)}) copy-start(f32[2,128,128]{2,1,0:T(8,128)} %param.15) | copy-start | bytes 393220
  134.4 2.1 %copy-start.6 = (f32[2,512]{1,0:T(2,128)S(1)}, f32[2,512]{1,0:T(2,128)}, u32[]{:S(2)}) copy-start(f32[2,512]{1,0:T(2,128)} %get-tuple-element.8) | copy-start | bytes 12292
  134.4 2.1 %copy-start.8 = (f32[2]{0:T(128)S(1)}, f32[2]{0:T(128)}, u32[]{:S(2)}) copy-start(f32[2]{0:T(128)} %get-tuple-element.5) | copy-start | bytes 28
  138.1 4.1 %copy-start.10 = (f32[512]{0:T(512)S(1)}, f32[512]{0:T(512)}, u32[]{:S(2)}) copy-start(f32[512]{0:T(512)} %copy-done.9) | copy-start | bytes 6148
  142.2 34.4 %copy-start.2 = (bf16[512,512]{1,0:T(8,128)(2,1)S(1)}, bf16[512,512]{1,0:T(8,128)(2,1)}, u32[]{:S(2)}) copy-start(bf16[512,512]{1,0:T(8,128)(2,1)} %param.8) | copy-start | bytes 1572868
Sparse Core Ops, SparseCore 0:
  9.2 38.8 all-gather.4
  60.8 73.6 all-gather.8
  147.4 29.1 all-gather.6
where the time goes:
time: 187 us
  waiting for transfers between devices  135 us (72%)
  matrix products  26.3 us (14%)
  between operations  13.3 us (7%)
  other arithmetic  9.55 us (5%)
  local copies, waits for them, and re-layouts  2.27 us (1%)
    all_gather x1, waiting for transfers between devices, per_device(): lax.all_gather(local_state[None].astype(jnp.bfloat16), 'seq', axis=0, til...  66.4 us
    all_gather x1, waiting for transfers between devices, per_device(): gathered = lax.all_gather(tokens, 'tp', axis=1, tiled=True)  38.8 us
    all_gather x1, waiting for transfers between devices, per_device(): lax.all_gather(hidden, 'tp', axis=1, tiled=True)  29.4 us
    dot_general x4, matrix products, per_device(): jnp.dot(gathered, weight, preferred_element_type=jnp.float32)  17.1 us
  transfers between devices with their start and end apart: 3, of which 3 were waited for; matrix products, arithmetic and copies ran while one was open for 5% of the time, Pallas kernels for 0%

commit v1 on v0

--- a/solution.py
+++ b/solution.py
@@ -42,8 +42,11 @@
     local_state = jnp.einsum(
         "hid,hie->hde", key_h.astype(jnp.float32) * tail_decay[:, :, None], value_f, precision=hi
     )
-    piece = lax.all_gather(
-        local_state[None].astype(jnp.bfloat16), "seq", axis=0, tiled=True
+    piece = jnp.concatenate(
+        lax.all_to_all(
+            jnp.stack([local_state[None].astype(jnp.bfloat16)] * lax.axis_size("seq")), "seq", 0, 0
+        ),
+        axis=0,
     ).astype(jnp.float32)
     count = piece.shape[0]
     source = jnp.arange(count)

time: 187 us -> 170 us (0.909)
  waiting for transfers between devices: 135 us -> 107 us
  starting transfers between devices: 0.08 us -> 9.74 us
    all_gather x1 -> x0, waiting for transfers between devices: 66.4 us -> none  [per_device(): lax.all_gather(local_state[None].astype(jnp.bfloat16), 'seq', axis=0, til...]
    all_to_all x0 -> x1, waiting for transfers between devices: none -> 41.5 us  [per_device(): lax.all_to_all(jnp.stack([local_state[None].astype(jnp.bfloat16)] * lax.a...]
    all_to_all x0 -> x1, starting transfers between devices: none -> 9.7 us  [per_device(): lax.all_to_all(jnp.stack([local_state[None].astype(jnp.bfloat16)] * lax.a...]
    all_gather x1, waiting for transfers between devices: 29.4 us -> 26.2 us  [per_device(): lax.all_gather(hidden, 'tp', axis=1, tiled=True)]
where the time goes in v1:
time: 170 us
  waiting for transfers between devices  107 us (63%)
  matrix products  25.7 us (15%)
  between operations  13.6 us (8%)
  starting transfers between devices  9.74 us (6%)
  other arithmetic  9.62 us (6%)
  local copies, waits for them, and re-layouts  3.73 us (2%)
    all_to_all x1, waiting for transfers between devices, per_device(): lax.all_to_all(jnp.stack([local_state[None].astype(jnp.bfloat16)] * lax.a...  41.5 us
    all_gather x1, waiting for transfers between devices, per_device(): gathered = lax.all_gather(tokens, 'tp', axis=1, tiled=True)  38.8 us
    all_gather x1, waiting for transfers between devices, per_device(): lax.all_gather(hidden, 'tp', axis=1, tiled=True)  26.2 us
    dot_general x4, matrix products, per_device(): jnp.dot(gathered, weight, preferred_element_type=jnp.float32)  17.1 us
    all_to_all x1, starting transfers between devices, per_device(): lax.all_to_all(jnp.stack([local_state[None].astype(jnp.bfloat16)] * lax.a...  9.7 us
    dot_general x1, matrix products, per_device(): jnp.dot(lax.all_gather(hidden, 'tp', axis=1, tiled=True), w_out, preferre...  3.66 us
  transfers between devices with their start and end apart: 3, of which 3 were waited for; matrix products, arithmetic and copies ran while one was open for 5% of the time, Pallas kernels for 0%

profile of v1, /device:TPU:1, one launch (start us, length us, event | category | flops | bytes accessed | tf_op | source)
XLA Modules:
  0.0 169.6 jit_solution(9894621198003400832)
XLA Ops:
  6.5 0.0 copy-start
  6.5 0.0 all-gather.3.cloned.1.call-start
  6.5 0.7 all-gather.3.cloned.1.call-update
  7.3 1.3 multiply_exponential_fusion.2
  8.6 0.0 copy-start.7
  8.6 0.7 multiply_exponential_fusion
  9.3 38.8 %all-gather.3.cloned.1.call-done = bf16[512,4096]{1,0:T(8,128)(2,1)} async-done(((bf16[512,512]{1,0:T(8,128)(2,1)}), bf16[512,4096]{1,0:T(8,128)(2,1)}) %all-gather.3.cloned.1.call-update) | async-done | bytes 4194320 | tf_op jit(solution)/shard_map/all_gather | solution.py:16
  48.1 0.0 copy-start.1
  48.1 3.2 %multiply_reduce_fusion = f32[512]{0:T(512)S(1)} fusion(bf16[512,4096]{1,0:T(8,128)(2,1)} %all-gather.3.cloned.1.call-done), kind=kLoop, calls=%fused_computation | loop fusion | flops 6290944 | bytes 4196352 | tf_op jit(solution)/shard_map/reduce_sum | solution.py:18
  51.3 0.2 copy-done.1
  51.5 0.0 copy-start.9
  51.5 2.9 %fusion.4 = bf16[512,256]{0,1:T(8,128)(2,1)S(1)} fusion(bf16[512,4096]{1,0:T(8,128)(2,1)S(1)} %copy-done.1, bf16[4096,256]{1,0:T(8,128)(2,1)} %param.11, f32[512]{0:T(512)S(1)} %add_rsqrt_fusion), kind=kOutput, calls=%fused_computation.12 | convolution fusion | flops 1074003968 | bytes 6555648 | tf_op jit(solution)/shard_map/dot_general | solution.py:20
  54.5 0.0 copy-start.4
  54.5 0.2 copy.15
  54.6 4.2 %multiply_convert_fusion.1 = bf16[512,256]{0,1:T(8,128)(2,1)S(1)} fusion(bf16[512,4096]{1,0:T(8,128)(2,1)} %all-gather.3.cloned.1.call-done, bf16[4096,256]{1,0:T(8,128)(2,1)} %param.10, f32[512]{0:T(512)S(1)} %add_rsqrt_fusion), kind=kOutput, calls=%fused_computation.29 | convolution fusion | flops 1074528256 | bytes 6555648 | tf_op jit(solution)/shard_map/dot_general | solution.py:20
  58.9 0.0 copy-done.4
  58.9 0.0 copy-start.3
  58.9 0.4 convolution_convert_fusion
  59.3 0.3 copy-done.3
  59.6 1.8 %stack.2 = bf16[32,1,2,128,128]{4,3,2,1,0:T(8,128)(2,1)} broadcast(bf16[2,128,128]{2,1,0:T(8,128)(2,1)S(1)} %convolution_convert_fusion), dimensions={2,3,4} | broadcast | bytes 2162688 | tf_op jit(solution)/shard_map/stack | solution.py:47
  61.5 9.7 %all-to-all-start = ((bf16[32,1,2,128,128]{4,3,2,1,0:T(8,128)(2,1)}), bf16[32,1,2,128,128]{4,3,2,1,0:T(8,128)(2,1)}, u32[]{:S(2)}, u32[]{:S(2)}) async-start(bf16[32,1,2,128,128]{4,3,2,1,0:T(8,128)(2,1)} %stack.2), calls=%async_computation | async-start | bytes 4194304 | tf_op jit(solution)/shard_map/all_to_all | solution.py:46
  71.2 0.0 all-gather.5.cloned.1.call-start
  71.3 0.0 copy-done.7
  71.3 0.1 exponential_select_fusion
  71.4 1.0 broadcast_compare_fusion
  72.3 0.2 subtract_select_fusion
  72.5 0.0 copy-done.9
  72.5 4.9 %multiply_convert_fusion.2 = bf16[512,256]{0,1:T(8,128)(2,1)} fusion(bf16[512,4096]{1,0:T(8,128)(2,1)} %all-gather.3.cloned.1.call-done, bf16[4096,256]{1,0:T(8,128)(2,1)} %param.9, f32[512]{0:T(512)S(1)} %add_rsqrt_fusion), kind=kOutput, calls=%fused_computation.30 | convolution fusion | flops 1074528256 | bytes 6555648 | tf_op jit(solution)/shard_map/dot_general | solution.py:20
  77.5 0.0 copy-start.5
  77.5 1.2 copy.14
  78.6 41.5 %all-to-all-done = bf16[32,1,2,128,128]{4,3,2,1,0:T(8,128)(2,1)} async-done(((bf16[32,1,2,128,128]{4,3,2,1,0:T(8,128)(2,1)}), bf16[32,1,2,128,128]{4,3,2,1,0:T(8,128)(2,1)}, u32[]{:S(2)}, u32[]{:S(2)}) %all-to-all-start) | async-done | bytes 2097184 | tf_op jit(solution)/shard_map/all_to_all | solution.py:46
  120.1 0.0 copy-start.6
  120.1 0.0 copy-start.8
  120.1 2.1 %fusion = f32[2,128,128]{2,1,0:T(8,128)S(1)} fusion(bf16[32,1,2,128,128]{4,3,2,1,0:T(8,128)(2,1)} %all-to-all-done, f32[32,2]{1,0:T(8,128)S(1)} %exponential_select_fusion), kind=kLoop, calls=%fused_computation.2 | loop fusion | flops 3112960 | bytes 2228480 | tf_op jit(solution)/shard_map/reduce_sum | solution.py:58
  122.2 0.0 copy-done.5
  122.2 0.0 copy-done.6
  122.2 0.0 copy-done.8
  122.2 1.6 fusion.12
  123.8 3.0 %multiply_reduce_fusion.1 = (f32[2,512]{1,0:T(2,128)S(1)}, f32[2,512,128]{1,2,0:T(8,128)}) fusion(f32[2,512,128]{1,2,0:T(8,128)} %fusion.12, bf16[2,512,128]{1,2,0:T(8,128)(2,1)} %bitcast.46, bf16[2,512,128]{1,2,0:T(8,128)(2,1)} %bitcast.44, f32[512,512]{1,0:T(8,128)S(1)} %subtract_select_fusion, f32[2]{0:T(128)} %copy-done.7, ...), kind=kOutput, calls=%fused_computation.22 | convolution fusion | flops 270924800 | bytes 3149832 | tf_op jit(solution)/shard_map/hij,hje->hie/dot_general | solution.py:39
  126.8 1.1 bitcast_multiply_fusion.1
  127.9 0.0 copy-done.10
  127.9 0.0 copy-start.2
  127.9 5.0 %fusion.9 = bf16[512,256]{0,1:T(8,128)(2,1)} fusion(f32[512,2,128]{0,2,1:T(8,128)S(1)} %bitcast_multiply_fusion.1, bf16[512,4096]{1,0:T(8,128)(2,1)} %all-gather.3.cloned.1.call-done, bf16[4096,256]{1,0:T(8,128)(2,1)} %param.12, f32[512]{0:T(512)S(1)} %copy-done.10), kind=kOutput, calls=%fused_computation.20 | convolution fusion | flops 1074659328 | bytes 7079936 | tf_op jit(solution)/shard_map/dot_general | solution.py:20
  132.9 0.0 all-gather.5.cloned.1.call-update
  132.9 26.2 %all-gather.5.cloned.1.call-done = bf16[512,2048]{0,1:T(8,128)(2,1)} async-done(((bf16[512,256]{0,1:T(8,128)(2,1)}), bf16[512,2048]{0,1:T(8,128)(2,1)}) %all-gather.5.cloned.1.call-update) | async-done | bytes 2097168 | tf_op jit(solution)/shard_map/all_gather | solution.py:70
  159.1 0.0 copy-done
  159.1 0.0 copy-done.2
  159.1 3.7 %fusion.2 = bf16[512,512]{1,0:T(8,128)(2,1)} fusion(bf16[512,2048]{0,1:T(8,128)(2,1)} %all-gather.5.cloned.1.call-done, bf16[2048,512]{1,0:T(8,128)(2,1)S(1)} %copy-done, bf16[512,512]{1,0:T(8,128)(2,1)S(1)} %copy-done.2), kind=kOutput, calls=%fused_computation.6 | convolution fusion | flops 1074528256 | bytes 5242880 | tf_op jit(solution)/shard_map/dot_general | solution.py:69
  (7 shorter events, 0.0 us)
Async XLA Ops:
  6.5 152.5 %copy-start = (bf16[2048,512]{1,0:T(8,128)(2,1)S(1)}, bf16[2048,512]{1,0:T(8,128)(2,1)}, u32[]{:S(2)}) copy-start(bf16[2048,512]{1,0:T(8,128)(2,1)} %param.13) | copy-start | bytes 6291460
  6.5 41.5 %all-gather.3.cloned.1.call-start = ((), (), s32[]{:S(2)}) async-start(), calls=%async_computation.1 | async-start | bytes 4718592 | tf_op jit(solution)/shard_map/all_gather | solution.py:16
  8.6 62.7 %copy-start.7 = (f32[2]{0:T(128)}, f32[2]{0:T(128)S(1)}, u32[]{:S(2)}) copy-start(f32[2]{0:T(128)S(1)} %get-tuple-element.6) | copy-start | bytes 28
  48.1 3.4 %copy-start.1 = (bf16[512,4096]{1,0:T(8,128)(2,1)S(1)}, bf16[512,4096]{1,0:T(8,128)(2,1)}, u32[]{:S(2)}) copy-start(bf16[512,4096]{1,0:T(8,128)(2,1)} %all-gather.3.cloned.1.call-done) | copy-start | bytes 12582916
  51.5 21.0 %copy-start.9 = (f32[512]{0:T(512)}, f32[512]{0:T(512)S(1)}, u32[]{:S(2)}) copy-start(f32[512]{0:T(512)S(1)} %add_rsqrt_fusion) | copy-start | bytes 6148
  54.5 4.4 %copy-start.4 = (bf16[512,256]{0,1:T(8,128)(2,1)}, bf16[512,256]{0,1:T(8,128)(2,1)S(1)}, u32[]{:S(2)}) copy-start(bf16[512,256]{0,1:T(8,128)(2,1)S(1)} %fusion.4) | copy-start | bytes 786436
  58.9 0.7 copy-start.3
  61.5 58.6 %all-to-all-start = ((bf16[32,1,2,128,128]{4,3,2,1,0:T(8,128)(2,1)}), bf16[32,1,2,128,128]{4,3,2,1,0:T(8,128)(2,1)}, u32[]{:S(2)}, u32[]{:S(2)}) async-start(bf16[32,1,2,128,128]{4,3,2,1,0:T(8,128)(2,1)} %stack.2), calls=%async_computation | async-start | bytes 4194304 | tf_op jit(solution)/shard_map/all_to_all | solution.py:46
  71.2 87.9 %all-gather.5.cloned.1.call-start = ((), (), s32[]{:S(2)}) async-start(), calls=%async_computation.2 | async-start | bytes 2359296 | tf_op jit(solution)/shard_map/all_gather | solution.py:70
  77.5 44.7 %copy-start.5 = (f32[2,128,128]{2,1,0:T(8,128)S(1)}, f32[2,128,128]{2,1,0:T(8,128)}, u32[]{:S(2)}) copy-start(f32[2,128,128]{2,1,0:T(8,128)} %param.15) | copy-start | bytes 393220
  120.1 2.1 %copy-start.6 = (f32[2,512]{1,0:T(2,128)S(1)}, f32[2,512]{1,0:T(2,128)}, u32[]{:S(2)}) copy-start(f32[2,512]{1,0:T(2,128)} %get-tuple-element.8) | copy-start | bytes 12292
  120.1 2.1 %copy-start.8 = (f32[2]{0:T(128)S(1)}, f32[2]{0:T(128)}, u32[]{:S(2)}) copy-start(f32[2]{0:T(128)} %get-tuple-element.5) | copy-start | bytes 28
  123.8 4.1 %copy-start.10 = (f32[512]{0:T(512)S(1)}, f32[512]{0:T(512)}, u32[]{:S(2)}) copy-start(f32[512]{0:T(512)} %copy-done.9) | copy-start | bytes 6148
  127.9 31.2 %copy-start.2 = (bf16[512,512]{1,0:T(8,128)(2,1)S(1)}, bf16[512,512]{1,0:T(8,128)(2,1)}, u32[]{:S(2)}) copy-start(bf16[512,512]{1,0:T(8,128)(2,1)} %param.8) | copy-start | bytes 1572868
Sparse Core Ops, SparseCore 0:
  9.2 38.8 all-gather.2
  133.0 25.9 all-gather.4
